TPU v7x, 32 devices: a whole 2x2x4 slice. The times are simulated.
32 devices in a mesh: clip: 2 (over y), tile: 4 (over z), tm: 2 (over x), chan: 2 (over core).
Axes of the slice: x: 2, y: 2, z: 4, core: 2. Of those that a mesh axis runs over, the one named last changes fastest.
Arguments:
- latent: bfloat16 [8, 8, 256, 128], P(('clip', 'tm'), 'tile', 'chan'), parts along dimension 0
- norm1_gain: float32 [256], P('chan'), may hold values from 0.25 to 1.75
- norm1_bias: float32 [256], P('chan'), may hold values from -3 to 3
- conv1_weight: bfloat16 [3, 3, 3, 256, 256], P(None, None, None, None, 'chan'), may hold values from -0.078125 to 0.078125
- conv1_bias: float32 [256], P('chan'), may hold values from -3 to 3
- norm2_gain: float32 [256], P('chan'), may hold values from 0.25 to 1.75
- norm2_bias: float32 [256], P('chan'), may hold values from -3 to 3
- conv2_weight: bfloat16 [3, 3, 3, 256, 256], P(None, None, None, None, 'chan'), may hold values from -0.078125 to 0.078125
- conv2_bias: float32 [256], P('chan'), may hold values from -3 to 3
Outputs:
- upsampled: bfloat16 [8, 16, 64, 256], P(('clip', 'tm'), 'tile', 'chan'), parts along dimension 0
There are 2 independent parts, one for each index of `clip`. A program takes and returns all parts, laid end to end along the dimension named above; an argument that names none is the same for every part. Nothing has to cross between parts.
All inputs are finite; a program needn't handle non-finite values.
Results may differ from a plain program's by a relative error of at most 0.0026.
Values may be sent and summed in bfloat16 or wider, within the bound.
A program may use at most 64 MiB of HBM per device.

v0:
```python
import jax
import jax.numpy as jnp
from jax import lax
from jax.sharding import PartitionSpec as P

C = 256
GROUPS = 32


def carried_in(part, axis, combine, identity):
    place = lax.axis_index(axis)
    gathered = jax.tree.map(lambda a: lax.all_gather(a, axis), part)
    state = jax.tree.map(lambda a, e: jnp.zeros_like(a) + jnp.asarray(e, a.dtype), part, identity)

    def one(lap, state):
        return combine(
            state, jax.tree.map(lambda a: lax.dynamic_index_in_dim(a, lap, 0, False), gathered)
        )

    return lax.fori_loop(0, place, one, state)


def passed_along(value, axis, steps):
    count = lax.axis_size(axis)
    initial, last = (max(0, -steps), min(count, count - steps))
    return lax.ppermute(value, axis, [(source, source + steps) for source in range(initial, last)])


def padded_2(cells, sides, width):
    for axis, dim in sides:
        count = lax.axis_size(axis)
        ends = count - 1
        head = lax.slice_in_dim(cells, 0, width, axis=dim)
        tail = lax.slice_in_dim(cells, cells.shape[dim] - width, cells.shape[dim], axis=dim)
        cells = jnp.concatenate(
            [
                lax.ppermute(tail, axis, [(i, (i + 1) % count) for i in range(ends)]),
                cells,
                lax.ppermute(head, axis, [((i + 1) % count, i) for i in range(ends)]),
            ],
            axis=dim,
        )
    return cells


def add_pair(earlier, later):
    return (earlier[0] + later[0], earlier[1] + later[1])


def causal_norm(field, gain, bias):
    frames, height, channels, columns = field.shape
    size = C // GROUPS
    local_groups = channels // size
    parts = field.reshape(frames, height, local_groups, size, columns)
    totals = jnp.sum(parts, axis=(1, 3, 4))
    squares = jnp.sum(parts * parts, axis=(1, 3, 4))
    totals, squares = lax.psum((totals, squares), "tile")
    run_totals = jnp.cumsum(totals, axis=0)
    run_squares = jnp.cumsum(squares, axis=0)
    empty = jnp.zeros((local_groups,), jnp.float32)
    before = carried_in((run_totals[-1], run_squares[-1]), "tm", add_pair, (empty, empty))
    run_totals = run_totals + before[0][None, :]
    run_squares = run_squares + before[1][None, :]
    frame_index = (jnp.arange(frames, dtype=jnp.int32) + lax.axis_index("tm") * frames).astype(
        jnp.float32
    )
    count = (frame_index + 1.0) * float(height * lax.axis_size("tile") * size * columns)
    mean = run_totals / count[:, None]
    var = run_squares / count[:, None] - mean * mean
    scale = 1.0 / jnp.sqrt(var + 1e-06)
    normed = (parts - mean[:, None, :, None, None]) * scale[:, None, :, None, None]
    normed = normed.reshape(frames, height, channels, columns)
    return normed * gain[None, None, :, None] + bias[None, None, :, None]


def extend(field):
    previous = passed_along(field, "tm", 1)
    opening = jnp.broadcast_to(field[0:1], previous.shape)
    previous = jnp.where(lax.axis_index("tm") == 0, opening, previous)
    timed = jnp.concatenate([previous, field], axis=0)
    return padded_2(timed, (("tile", 1),), 1)


def causal_conv(field, weight, bias):
    frames, height, channels, columns = field.shape
    gathered = lax.all_gather(field, "chan", axis=2, tiled=True)
    extended = extend(gathered)
    padded = jnp.pad(extended, ((0, 0), (0, 0), (0, 0), (1, 1)))
    total = jnp.zeros((frames, height, weight.shape[4], columns), jnp.float32)
    for depth_tap in range(3):
        for row_tap in range(3):
            slab = padded[depth_tap : depth_tap + frames, row_tap : row_tap + height]
            stacked = jnp.stack(
                [slab[..., shift_tap : shift_tap + columns] for shift_tap in range(3)], axis=0
            )
            total = total + jnp.einsum(
                "kfrcw,kcd->frdw",
                stacked,
                weight[depth_tap, row_tap],
                preferred_element_type=jnp.float32,
            )
    return total + bias[None, None, :, None]


def shards(
    latent,
    norm1_gain,
    norm1_bias,
    conv1_weight,
    conv1_bias,
    norm2_gain,
    norm2_bias,
    conv2_weight,
    conv2_bias,
):
    source = latent.astype(jnp.float32)
    first = jax.nn.silu(causal_norm(source, norm1_gain, norm1_bias)).astype(jnp.bfloat16)
    hidden = causal_conv(first, conv1_weight, conv1_bias)
    second = jax.nn.silu(causal_norm(hidden, norm2_gain, norm2_bias)).astype(jnp.bfloat16)
    mixed = source + causal_conv(second, conv2_weight, conv2_bias)
    frames, height, channels, columns = mixed.shape
    shaped = mixed.reshape(frames, height, channels // 4, 2, 2, columns)
    shaped = jnp.transpose(shaped, (0, 1, 3, 2, 5, 4))
    return shaped.reshape(frames, 2 * height, channels // 4, 2 * columns).astype(jnp.bfloat16)


def solution(mesh):
    return jax.shard_map(
        shards,
        mesh=mesh,
        in_specs=(
            P(("clip", "tm"), "tile", "chan", None),
            P("chan"),
            P("chan"),
            P(None, None, None, None, "chan"),
            P("chan"),
            P("chan"),
            P("chan"),
            P(None, None, None, None, "chan"),
            P("chan"),
        ),
        out_specs=P(("clip", "tm"), "tile", "chan", None),
        check_vma=False,
    )
```

profile of v0, /device:TPU:0, one launch (start us, length us, event | category | flops | bytes accessed | tf_op | source)
XLA Modules:
  0.0 104.3 jit_solution(5707471050014046221)
XLA Ops:
  0.0 1.0 copy.90
  1.4 13.5 %all-reduce.3 = (f32[2,16]{1,0:T(2,128)S(1)}, f32[2,16]{1,0:T(2,128)S(1)}) all-reduce(f32[2,16]{1,0:T(2,128)S(1)} %reduce_sum.51, f32[2,16]{1,0:T(2,128)S(1)} %reduce_sum.54), channel_id=1, replica_groups=mesh['clip'=2,'tile'=4,'tm'=2,'chan'=2] {'tile'}, use_global_device_ids=true, to_apply=%region_2.0 | all-reduce | flops 64 | bytes 512 | tf_op jit(solution)/shard_map/psum | solution.py:57
  15.0 4.2 %all-gather = f32[2,1,16]{2,1,0:T(1,128)S(1)} all-gather(f32[1,1,16]{2,1,0:T(1,128)S(1)} %slice_bitcast_fusion.53), channel_id=1, replica_groups=mesh['clip'=2,'tile'=4,'tm'=2,'chan'=2] {'tm'}, dimensions={0}, use_global_device_ids=true | all-gather | bytes 192 | tf_op jit(solution)/shard_map/all_gather | solution.py:12
  19.2 4.2 %all-gather.1 = f32[2,1,16]{2,1,0:T(1,128)S(1)} all-gather(f32[1,1,16]{2,1,0:T(1,128)S(1)} %slice_bitcast_fusion.52), channel_id=1, replica_groups=mesh['clip'=2,'tile'=4,'tm'=2,'chan'=2] {'tm'}, dimensions={0}, use_global_device_ids=true | all-gather | bytes 192 | tf_op jit(solution)/shard_map/all_gather | solution.py:12
  23.9 0.8 fusion.52
  24.7 2.0 %all_gather.20 = bf16[2,2,256,128]{2,3,1,0:T(8,128)(2,1)S(1)} all-gather(bf16[2,2,128,128]{2,3,1,0:T(8,128)(2,1)S(1)} %fusion.52), channel_id=1, replica_groups=mesh['clip'=2,'tile'=4,'tm'=2,'chan'=2] {'chan'}, dimensions={2}, use_global_device_ids=true | all-gather | bytes 393216 | tf_op jit(solution)/shard_map/all_gather | solution.py:86
  26.7 3.4 %collective-permute-start = (bf16[2,2,256,128]{2,3,1,0:T(8,128)(2,1)S(1)}, bf16[2,2,256,128]{2,3,1,0:T(8,128)(2,1)S(1)}, u32[]{:S(2)}, u32[]{:S(2)}) collective-permute-start(bf16[2,2,256,128]{2,3,1,0:T(8,128)(2,1)S(1)} %all_gather.20), channel_id=1, source_target_pairs={{0,2},{1,3},{4,6},{5,7},{8,10},{9,11},{12,14},{13,15},{16,18},{17,... | collective-permute-start | bytes 786440 | tf_op jit(solution)/shard_map/ppermute | solution.py:26
  30.1 5.8 %collective-permute-done = bf16[2,2,256,128]{2,3,1,0:T(8,128)(2,1)S(1)} collective-permute-done((bf16[2,2,256,128]{2,3,1,0:T(8,128)(2,1)S(1)}, bf16[2,2,256,128]{2,3,1,0:T(8,128)(2,1)S(1)}, u32[]{:S(2)}, u32[]{:S(2)}) %collective-permute-start) | collective-permute-done | bytes 262176 | tf_op jit(solution)/shard_map/ppermute | solution.py:26
  36.0 1.3 %collective-permute-start.1 = (bf16[4,1,256,128]{2,3,1,0:T(8,128)(2,1)S(1)}, bf16[4,1,256,128]{2,3,1,0:T(8,128)(2,1)S(1)}, u32[]{:S(2)}, u32[]{:S(2)}) collective-permute-start(bf16[4,1,256,128]{2,3,1,0:T(8,128)(2,1)S(1)} %get-tuple-element.171), channel_id=1, source_target_pairs={{0,4},{4,8},{8,12},{1,5},{5,9},{9,13},{2,6},{6,10},{10,14},{3,7},{... | collective-permute-start | bytes 786440 | tf_op jit(solution)/shard_map/ppermute | solution.py:37
  37.4 1.3 %collective-permute-start.2 = (bf16[4,1,256,128]{2,3,1,0:T(8,128)(2,1)S(1)}, bf16[4,1,256,128]{2,3,1,0:T(8,128)(2,1)S(1)}, u32[]{:S(2)}, u32[]{:S(2)}) collective-permute-start(bf16[4,1,256,128]{2,3,1,0:T(8,128)(2,1)S(1)} %get-tuple-element.172), channel_id=1, source_target_pairs={{4,0},{8,4},{12,8},{5,1},{9,5},{13,9},{6,2},{10,6},{14,10},{7,3},{... | collective-permute-start | bytes 786440 | tf_op jit(solution)/shard_map/ppermute | solution.py:39
  38.7 3.9 %collective-permute-done.1 = bf16[4,1,256,128]{2,3,1,0:T(8,128)(2,1)S(1)} collective-permute-done((bf16[4,1,256,128]{2,3,1,0:T(8,128)(2,1)S(1)}, bf16[4,1,256,128]{2,3,1,0:T(8,128)(2,1)S(1)}, u32[]{:S(2)}, u32[]{:S(2)}) %collective-permute-start.1) | collective-permute-done | bytes 262176 | tf_op jit(solution)/shard_map/ppermute | solution.py:37
  42.6 4.1 %collective-permute-done.2 = bf16[4,1,256,128]{2,3,1,0:T(8,128)(2,1)S(1)} collective-permute-done((bf16[4,1,256,128]{2,3,1,0:T(8,128)(2,1)S(1)}, bf16[4,1,256,128]{2,3,1,0:T(8,128)(2,1)S(1)}, u32[]{:S(2)}, u32[]{:S(2)}) %collective-permute-start.2) | collective-permute-done | bytes 262176 | tf_op jit(solution)/shard_map/ppermute | solution.py:39
  46.9 0.4 fusion.18
  47.4 0.8 slice_bitcast_fusion.44
  48.4 1.3 %copy-done.3 = bf16[3,3,3,256,128]{4,3,2,1,0:T(8,128)(2,1)S(1)} copy-done((bf16[3,3,3,256,128]{4,3,2,1,0:T(8,128)(2,1)S(1)}, bf16[3,3,3,256,128]{4,3,2,1,0:T(8,128)(2,1)}, u32[]{:S(2)}) %copy-start.3) | copy-done | bytes 1769496
  53.3 0.4 multiply_reduce_fusion
  54.1 8.8 %all-reduce.2 = (f32[2,16]{1,0:T(2,128)S(1)}, f32[2,16]{1,0:T(2,128)S(1)}) all-reduce(f32[2,16]{1,0:T(2,128)S(1)} %reduce_sum.72, f32[2,16]{1,0:T(2,128)S(1)} %reduce_sum.75), channel_id=1, replica_groups=mesh['clip'=2,'tile'=4,'tm'=2,'chan'=2] {'tile'}, use_global_device_ids=true, to_apply=%region_12.13 | all-reduce | flops 64 | bytes 512 | tf_op jit(solution)/shard_map/psum | solution.py:57
  63.0 4.7 %all-gather.2 = f32[2,1,16]{2,1,0:T(1,128)S(1)} all-gather(f32[1,1,16]{2,1,0:T(1,128)S(1)} %slice_bitcast_fusion.51), channel_id=1, replica_groups=mesh['clip'=2,'tile'=4,'tm'=2,'chan'=2] {'tm'}, dimensions={0}, use_global_device_ids=true | all-gather | bytes 192 | tf_op jit(solution)/shard_map/all_gather | solution.py:12
  67.7 4.2 %all-gather.3 = f32[2,1,16]{2,1,0:T(1,128)S(1)} all-gather(f32[1,1,16]{2,1,0:T(1,128)S(1)} %slice_bitcast_fusion.50), channel_id=1, replica_groups=mesh['clip'=2,'tile'=4,'tm'=2,'chan'=2] {'tm'}, dimensions={0}, use_global_device_ids=true | all-gather | bytes 192 | tf_op jit(solution)/shard_map/all_gather | solution.py:12
  72.5 2.0 %all_gather.23 = bf16[2,2,256,128]{2,3,1,0:T(8,128)(2,1)S(1)} all-gather(bf16[2,2,128,128]{2,3,1,0:T(8,128)(2,1)S(1)} %multiply_convert_fusion), channel_id=1, replica_groups=mesh['clip'=2,'tile'=4,'tm'=2,'chan'=2] {'chan'}, dimensions={2}, use_global_device_ids=true | all-gather | bytes 393216 | tf_op jit(solution)/shard_map/all_gather | solution.py:86
  74.5 4.0 %collective-permute-start.3 = (bf16[2,2,256,128]{2,3,1,0:T(8,128)(2,1)S(1)}, bf16[2,2,256,128]{2,3,1,0:T(8,128)(2,1)S(1)}, u32[]{:S(2)}, u32[]{:S(2)}) collective-permute-start(bf16[2,2,256,128]{2,3,1,0:T(8,128)(2,1)S(1)} %all_gather.23), channel_id=1, source_target_pairs={{0,2},{1,3},{4,6},{5,7},{8,10},{9,11},{12,14},{13,15},{16,18},{17,... | collective-permute-start | bytes 786440 | tf_op jit(solution)/shard_map/ppermute | solution.py:26
  78.5 5.8 %collective-permute-done.3 = bf16[2,2,256,128]{2,3,1,0:T(8,128)(2,1)S(1)} collective-permute-done((bf16[2,2,256,128]{2,3,1,0:T(8,128)(2,1)S(1)}, bf16[2,2,256,128]{2,3,1,0:T(8,128)(2,1)S(1)}, u32[]{:S(2)}, u32[]{:S(2)}) %collective-permute-start.3) | collective-permute-done | bytes 262176 | tf_op jit(solution)/shard_map/ppermute | solution.py:26
  84.4 3.4 %collective-permute-start.4 = (bf16[4,1,256,128]{2,3,1,0:T(8,128)(2,1)S(1)}, bf16[4,1,256,128]{2,3,1,0:T(8,128)(2,1)S(1)}, u32[]{:S(2)}, u32[]{:S(2)}) collective-permute-start(bf16[4,1,256,128]{2,3,1,0:T(8,128)(2,1)S(1)} %get-tuple-element.167), channel_id=1, source_target_pairs={{0,4},{4,8},{8,12},{1,5},{5,9},{9,13},{2,6},{6,10},{10,14},{3,7},{... | collective-permute-start | bytes 786440 | tf_op jit(solution)/shard_map/ppermute | solution.py:37
  87.8 1.3 %collective-permute-start.5 = (bf16[4,1,256,128]{2,3,1,0:T(8,128)(2,1)S(1)}, bf16[4,1,256,128]{2,3,1,0:T(8,128)(2,1)S(1)}, u32[]{:S(2)}, u32[]{:S(2)}) collective-permute-start(bf16[4,1,256,128]{2,3,1,0:T(8,128)(2,1)S(1)} %get-tuple-element.168), channel_id=1, source_target_pairs={{4,0},{8,4},{12,8},{5,1},{9,5},{13,9},{6,2},{10,6},{14,10},{7,3},{... | collective-permute-start | bytes 786440 | tf_op jit(solution)/shard_map/ppermute | solution.py:39
  89.2 3.6 %collective-permute-done.4 = bf16[4,1,256,128]{2,3,1,0:T(8,128)(2,1)S(1)} collective-permute-done((bf16[4,1,256,128]{2,3,1,0:T(8,128)(2,1)S(1)}, bf16[4,1,256,128]{2,3,1,0:T(8,128)(2,1)S(1)}, u32[]{:S(2)}, u32[]{:S(2)}) %collective-permute-start.4) | collective-permute-done | bytes 262176 | tf_op jit(solution)/shard_map/ppermute | solution.py:37
  92.8 4.1 %collective-permute-done.5 = bf16[4,1,256,128]{2,3,1,0:T(8,128)(2,1)S(1)} collective-permute-done((bf16[4,1,256,128]{2,3,1,0:T(8,128)(2,1)S(1)}, bf16[4,1,256,128]{2,3,1,0:T(8,128)(2,1)S(1)}, u32[]{:S(2)}, u32[]{:S(2)}) %collective-permute-start.5) | collective-permute-done | bytes 262176 | tf_op jit(solution)/shard_map/ppermute | solution.py:39
  97.2 0.4 select_maximum_fusion
  97.6 0.9 slice_bitcast_fusion.23
  98.6 0.5 copy-done.4
  102.1 0.4 convolution_bitcast_fusion
  103.0 0.4 copy.137
  103.4 0.8 copy.138
  (83 shorter events, 9.8 us)
Async XLA Ops:
  26.7 9.3 %collective-permute-start = (bf16[2,2,256,128]{2,3,1,0:T(8,128)(2,1)S(1)}, bf16[2,2,256,128]{2,3,1,0:T(8,128)(2,1)S(1)}, u32[]{:S(2)}, u32[]{:S(2)}) collective-permute-start(bf16[2,2,256,128]{2,3,1,0:T(8,128)(2,1)S(1)} %all_gather.20), channel_id=1, source_target_pairs={{0,2},{1,3},{4,6},{5,7},{8,10},{9,11},{12,14},{13,15},{16,18},{17,... | collective-permute-start | bytes 786440 | tf_op jit(solution)/shard_map/ppermute | solution.py:26
  36.0 6.6 %collective-permute-start.1 = (bf16[4,1,256,128]{2,3,1,0:T(8,128)(2,1)S(1)}, bf16[4,1,256,128]{2,3,1,0:T(8,128)(2,1)S(1)}, u32[]{:S(2)}, u32[]{:S(2)}) collective-permute-start(bf16[4,1,256,128]{2,3,1,0:T(8,128)(2,1)S(1)} %get-tuple-element.171), channel_id=1, source_target_pairs={{0,4},{4,8},{8,12},{1,5},{5,9},{9,13},{2,6},{6,10},{10,14},{3,7},{... | collective-permute-start | bytes 786440 | tf_op jit(solution)/shard_map/ppermute | solution.py:37
  37.4 9.4 %collective-permute-start.2 = (bf16[4,1,256,128]{2,3,1,0:T(8,128)(2,1)S(1)}, bf16[4,1,256,128]{2,3,1,0:T(8,128)(2,1)S(1)}, u32[]{:S(2)}, u32[]{:S(2)}) collective-permute-start(bf16[4,1,256,128]{2,3,1,0:T(8,128)(2,1)S(1)} %get-tuple-element.172), channel_id=1, source_target_pairs={{4,0},{8,4},{12,8},{5,1},{9,5},{13,9},{6,2},{10,6},{14,10},{7,3},{... | collective-permute-start | bytes 786440 | tf_op jit(solution)/shard_map/ppermute | solution.py:39
  48.2 1.5 %copy-start.3 = (bf16[3,3,3,256,128]{4,3,2,1,0:T(8,128)(2,1)S(1)}, bf16[3,3,3,256,128]{4,3,2,1,0:T(8,128)(2,1)}, u32[]{:S(2)}) copy-start(bf16[3,3,3,256,128]{4,3,2,1,0:T(8,128)(2,1)} %param.16) | copy-start | bytes 5308420
  52.6 0.8 copy-start.5
  53.3 19.0 %copy-start = (f32[128]{0:T(128)S(1)}, f32[128]{0:T(128)}, u32[]{:S(2)}) copy-start(f32[128]{0:T(128)} %param.19) | copy-start | bytes 1540
  53.3 19.0 %copy-start.1 = (f32[128]{0:T(128)S(1)}, f32[128]{0:T(128)}, u32[]{:S(2)}) copy-start(f32[128]{0:T(128)} %param.18) | copy-start | bytes 1540
  74.5 9.8 %collective-permute-start.3 = (bf16[2,2,256,128]{2,3,1,0:T(8,128)(2,1)S(1)}, bf16[2,2,256,128]{2,3,1,0:T(8,128)(2,1)S(1)}, u32[]{:S(2)}, u32[]{:S(2)}) collective-permute-start(bf16[2,2,256,128]{2,3,1,0:T(8,128)(2,1)S(1)} %all_gather.23), channel_id=1, source_target_pairs={{0,2},{1,3},{4,6},{5,7},{8,10},{9,11},{12,14},{13,15},{16,18},{17,... | collective-permute-start | bytes 786440 | tf_op jit(solution)/shard_map/ppermute | solution.py:26
  84.4 8.4 %collective-permute-start.4 = (bf16[4,1,256,128]{2,3,1,0:T(8,128)(2,1)S(1)}, bf16[4,1,256,128]{2,3,1,0:T(8,128)(2,1)S(1)}, u32[]{:S(2)}, u32[]{:S(2)}) collective-permute-start(bf16[4,1,256,128]{2,3,1,0:T(8,128)(2,1)S(1)} %get-tuple-element.167), channel_id=1, source_target_pairs={{0,4},{4,8},{8,12},{1,5},{5,9},{9,13},{2,6},{6,10},{10,14},{3,7},{... | collective-permute-start | bytes 786440 | tf_op jit(solution)/shard_map/ppermute | solution.py:37
  87.8 9.1 %collective-permute-start.5 = (bf16[4,1,256,128]{2,3,1,0:T(8,128)(2,1)S(1)}, bf16[4,1,256,128]{2,3,1,0:T(8,128)(2,1)S(1)}, u32[]{:S(2)}, u32[]{:S(2)}) collective-permute-start(bf16[4,1,256,128]{2,3,1,0:T(8,128)(2,1)S(1)} %get-tuple-element.168), channel_id=1, source_target_pairs={{4,0},{8,4},{12,8},{5,1},{9,5},{13,9},{6,2},{10,6},{14,10},{7,3},{... | collective-permute-start | bytes 786440 | tf_op jit(solution)/shard_map/ppermute | solution.py:39
  97.6 1.5 %copy-start.4 = (bf16[3,3,3,256,128]{4,3,2,1,0:T(8,128)(2,1)S(1)}, bf16[3,3,3,256,128]{4,3,2,1,0:T(8,128)(2,1)}, u32[]{:S(2)}) copy-start(bf16[3,3,3,256,128]{4,3,2,1,0:T(8,128)(2,1)} %param.20) | copy-start | bytes 5308420
  102.1 0.7 copy-start.2
where the time goes:
time: 105 us; the launch traced here: 104 us
  blocking collectives  43.7 us (42%)
  waiting for transfers between devices  27.4 us (26%)
  starting transfers between devices  14.7 us (14%)
  local copies, waits for them, and re-layouts  7.53 us (7%)
  matrix products  6.68 us (6%)
  other arithmetic  3.81 us (4%)
    psum x2, blocking collectives, causal_norm(): totals, squares = lax.psum((totals, squares), 'tile')  22.3 us
    all_gather x4, blocking collectives, carried_in(): gathered = jax.tree.map(lambda a: lax.all_gather(a, axis), part)  17.3 us
    ppermute x2, waiting for transfers between devices, passed_along(): lax.ppermute(value, axis, [(source, source + steps) for source in range(i...  11.6 us
    ppermute x2, waiting for transfers between devices, padded_2(): lax.ppermute(head, axis, [((i + 1) % count, i) for i in range(ends)])  8.26 us
    ppermute x2, waiting for transfers between devices, padded_2(): lax.ppermute(tail, axis, [(i, (i + 1) % count) for i in range(ends)])  7.51 us
    ppermute x2, starting transfers between devices, passed_along(): lax.ppermute(value, axis, [(source, source + steps) for source in range(i...  7.4 us
    dot_general x18, matrix products, causal_conv(): jnp.einsum('kfrcw,kcd->frdw', stacked, weight[depth_tap, row_tap], prefer...  6.68 us
    ppermute x2, starting transfers between devices, padded_2(): lax.ppermute(tail, axis, [(i, (i + 1) % count) for i in range(ends)])  4.72 us
  transfers between devices with their start and end apart: 6, of which 6 were waited for; matrix products, arithmetic and copies ran while one was open for 0% of the time, Pallas kernels for 0%

commit v1 on v0

v1 whole, which is shorter than its diff:
```python
import functools

import jax
import jax.numpy as jnp
from jax import lax
from jax.experimental import pallas as pl
from jax.experimental.pallas import tpu as pltpu
from jax.sharding import PartitionSpec as P

MESH = pl.DeviceIdType.MESH
C = 256
GROUPS = 32
SIZE = C // GROUPS
F32 = jnp.float32
BF16 = jnp.bfloat16


def iota(shape, dim):
    return lax.broadcasted_iota(jnp.int32, shape, dim)


def column(row, n):
    wide = jnp.broadcast_to(row, (n, row.shape[-1]))
    return jnp.sum(jnp.where(iota(wide.shape, 0) == iota(wide.shape, 1), wide, 0.0), axis=1, keepdims=True)


def kernel(
    tiles,
    blocks,
    latent,
    n1g,
    n1b,
    w1,
    c1b,
    n2g,
    n2b,
    w2,
    c2b,
    out,
    w1v,
    w2v,
    w1t,
    w2t,
    lat,
    act1,
    hid,
    act2,
    mix,
    params,
    own_stats,
    stats,
    means,
    scales,
    w_sem,
    p_sem,
    x_send,
    z_send,
    d_send,
    a_recv,
    d_recv,
    hz_send,
    hd_send,
    h_recv,
    hd_recv,
    s_send,
    s_recv,
):
    cores = 2
    count_all = tiles * blocks * cores
    tm = lax.axis_index("tm")
    tile = lax.axis_index("tile")
    core = lax.axis_index("chan")
    other = 1 - core
    me = (tm * cores + core) * tiles + tile
    local = latent.shape[2]
    wide = latent.shape[3]
    groups = local // SIZE
    rows = latent.shape[1]

    def where_is(index):
        return {"tm": index // (cores * tiles), "chan": (index // tiles) % cores, "tile": index % tiles}

    load1 = pltpu.make_async_copy(w1, w1v, w_sem.at[0])
    load2 = pltpu.make_async_copy(w2, w2v, w_sem.at[1])
    load1.start()
    load2.start()

    barrier = pltpu.get_barrier_semaphore()

    def greet(step, carry):
        pl.semaphore_signal(
            barrier, inc=1, device_id=where_is(lax.rem(me + step, count_all)), device_id_type=MESH
        )
        return carry

    lax.fori_loop(1, count_all, greet, 0)
    for i, ref in enumerate((n1g, n1b, n2g, n2b, c1b)):
        params[core, i] = ref[...]
    lat[2, 1, core] = latent[:, 0]
    lat[2, 2, core] = latent[:, 1]
    pl.semaphore_wait(barrier, count_all - 1)

    def remote(src, dst, send, recv, **device):
        return pltpu.make_async_remote_copy(
            src_ref=src, dst_ref=dst, send_sem=send, recv_sem=recv, device_id=device, device_id_type=MESH
        )

    started = []

    def go(condition, copy):
        @pl.when(condition)
        def _():
            copy.start()

        started.append((condition, copy))

    always = core >= 0
    has_up = tile < tiles - 1
    has_down = tile > 0
    slots = [s for s in range(3) if blocks > 2 - s]
    before = [s for s in slots if s < 2]

    for s in reversed(before):
        for r in (0, 1):
            go(
                tm + (2 - s) < blocks,
                remote(latent.at[:, r], lat.at[s, 1 + r, core], x_send.at[s, r], a_recv.at[s, 1 + r],
                       tm=tm + (2 - s)),
            )
    go(has_up, remote(latent.at[:, 1], lat.at[2, 0, core], z_send.at[2, 0], a_recv.at[2, 0], tile=tile + 1))
    go(has_down, remote(latent.at[:, 0], lat.at[2, 3, core], z_send.at[2, 1], a_recv.at[2, 3], tile=tile - 1))
    for r in (0, 1):
        go(always, remote(latent.at[:, r], lat.at[2, 1 + r, core], d_send.at[2, 1 + r], d_recv.at[2, 1 + r],
                          chan=other))
    go(always, remote(params.at[core], params.at[core], p_sem.at[0], p_sem.at[1], chan=other))

    lanes = iota((groups, 128), 1)
    subs = iota((groups, 128), 0)

    def send_stats(which, field):
        row = jnp.zeros((1, 128), F32)
        for f in (0, 1):
            total = jnp.zeros((groups, wide), F32)
            square = jnp.zeros((groups, wide), F32)
            for r in (0, 1):
                v = field(f, r).reshape(groups, SIZE, wide)
                total = total + jnp.sum(v, axis=1)
                square = square + jnp.sum(v * v, axis=1)
            for kind, part in enumerate((total, square)):
                col = jnp.sum(part, axis=1, keepdims=True)
                at = kind * 2 * groups + f * groups
                row = row + jnp.sum(jnp.where(lanes == subs + at, col, 0.0), axis=0, keepdims=True)
        own_stats[which] = row
        stats[which, me] = row

        def send(step, carry):
            to = lax.rem(me + step, count_all)
            remote(own_stats.at[which], stats.at[which, me], s_send.at[which, to], s_recv.at[which, me],
                   **where_is(to)).start()
            return carry

        lax.fori_loop(1, count_all, send, 0)

    def wait_stats(which):
        def wait(step, carry):
            to = lax.rem(me + step, count_all)
            remote(own_stats.at[which], stats.at[which, to], s_send.at[which, to], s_recv.at[which, to],
                   **where_is(to)).wait()
            return carry

        lax.fori_loop(1, count_all, wait, 0)

    def make_norms(which, frames):
        ahead = frames // 2 - 1
        per_block = []
        for b in range(blocks):
            for c in range(cores):
                first = jnp.sum(stats[which, pl.ds((b * cores + c) * tiles, tiles)], axis=0)
                both = first + pltpu.roll(first, 128 - groups, 1)
                per_block.append((b, c, first, both))
        for e in range(frames):
            block = tm - ahead + e // 2
            later = jnp.logical_and(block >= 0, e % 2 == 1)
            block = jnp.maximum(block, 0)
            number = (block * 2 + later.astype(jnp.int32) + 1).astype(F32)
            count = number * float(rows * tiles * SIZE * wide)
            for c in range(cores):
                run = jnp.zeros((1, 128), F32)
                for b, cc, first, both in per_block:
                    if cc == c:
                        whole = jnp.logical_or(b < block, jnp.logical_and(b == block, later))
                        run = run + jnp.where(whole, both, jnp.where(b == block, first, 0.0))
                mean = run / count
                var = pltpu.roll(mean, 128 - 2 * groups, 1) - mean * mean
                scale = 1.0 / jnp.sqrt(var + 1e-06)
                diagonal = lanes == subs
                for ref, value in ((means, mean), (scales, scale)):
                    col = jnp.sum(jnp.where(diagonal, jnp.broadcast_to(value, lanes.shape), 0.0), axis=1,
                                  keepdims=True)
                    ref[e * cores + c] = jnp.broadcast_to(col, (groups, 128))

    def per_channel(ref, at):
        v = ref[at]
        return jnp.broadcast_to(v[:, None, :], (groups, SIZE, 128)).reshape(local, 128)

    def flip(src, dst):
        def one(j, carry):
            for i in range(3):
                for k in range(3):
                    dst[j, k * local:(k + 1) * local, i * C:(i + 1) * C] = src[i, j, k].T
            return carry

        lax.fori_loop(0, 3, one, 0)

    def silu(v):
        half = 0.5 * v
        return half + half * jnp.tanh(half)

    def conv(act, wt, o):
        acc = None
        for j in range(3):
            part = jnp.dot(
                wt[j], act[pl.ds(pl.multiple_of(o * C, C), 3 * C), j * wide:(j + 2) * wide],
                preferred_element_type=F32,
            )
            acc = part if acc is None else acc + part
        lane = iota((local, wide), 1)
        result = []
        for r in range(2):
            a = [acc[k * local:(k + 1) * local, r * wide:(r + 1) * wide] for k in range(3)]
            left = jnp.where(lane == 0, 0.0, pltpu.roll(a[0], 1, 1))
            right = jnp.where(lane == wide - 1, 0.0, pltpu.roll(a[2], wide - 1, 1))
            result.append(a[1] + left + right)
        return result

    send_stats(0, lambda f, r: latent[f, r].astype(F32))
    load1.wait()
    flip(w1v, w1t)

    def arrived(s, row, condition):
        got = remote(lat.at[s, row, core], lat.at[s, row, core], d_send.at[s, row], a_recv.at[s, row], chan=other)

        @pl.when(condition)
        def _():
            got.wait_recv()

        go(condition, remote(lat.at[s, row, core], lat.at[s, row, core], d_send.at[s, row], d_recv.at[s, row],
                             chan=other))

    arrivals = []
    for s in reversed(before):
        here = tm >= 2 - s
        for r in (0, 1):
            arrived(s, 1 + r, here)
            side, row, to = ((has_down, 3, tile - 1), (has_up, 0, tile + 1))[r]
            go(
                jnp.logical_and(here, side),
                remote(lat.at[s, 1 + r, core], lat.at[s, row, core], z_send.at[s, 1 - r], a_recv.at[s, row], tile=to),
            )
    for s in reversed(slots):
        here = tm >= 2 - s
        arrived(s, 0, jnp.logical_and(here, has_down))
        arrived(s, 3, jnp.logical_and(here, has_up))

    wait_stats(0)
    make_norms(0, 6)
    remote(params.at[core], params.at[other], p_sem.at[0], p_sem.at[1], chan=other).wait_recv()

    def row_here(row):
        return has_down if row == 0 else has_up if row == 3 else always

    for s in reversed(slots):
        for row in range(4):
            @pl.when(jnp.logical_and(tm >= 2 - s, row_here(row)))
            def _(s=s, row=row):
                remote(lat.at[s, row, core], lat.at[s, row, other], d_send.at[s, row], d_recv.at[s, row],
                       chan=other).wait_recv()

    def norm1(step, carry):
        e, c = step // cores, step % cores
        s, f = e // 2, e % 2
        f = jnp.where(tm - 2 + s < 0, 0, f)
        s = jnp.maximum(s, 2 - tm)
        mean = per_channel(means, step)
        gain = per_channel(scales, step) * column(params[c, 0], local)
        bias = column(params[c, 1], local)
        for row in range(4):
            v = lat[s, row, c, f].astype(F32)
            v = silu((v - mean) * gain + bias)
            v = jnp.where(row_here(row), v, 0.0)
            act1[pl.ds(pl.multiple_of(step * local, local), local), row * wide:(row + 1) * wide] = v.astype(BF16)
        return carry

    lax.fori_loop(0, 6 * cores, norm1, 0)

    def conv1(o, carry):
        for r, h in enumerate(conv(act1, w1t, o)):
            hid[1 + r, core, o] = h.astype(BF16)

            @pl.when(o >= 2)
            def _():
                mix[(o - 2) * 2 + r] = h
        return carry

    lax.fori_loop(0, 4, conv1, 0)

    go(has_up, remote(hid.at[2, core], hid.at[0, core], hz_send.at[0], h_recv.at[0], tile=tile + 1))
    go(has_down, remote(hid.at[1, core], hid.at[3, core], hz_send.at[1], h_recv.at[1], tile=tile - 1))
    for r in (1, 2):
        go(always, remote(hid.at[r, core], hid.at[r, core], hd_send.at[r], hd_recv.at[r], chan=other))
    bias1 = column(c1b[...], local)
    send_stats(1, lambda f, r: mix[f * 2 + r] + bias1)
    load2.wait()
    flip(w2v, w2t)
    for at, row, side in ((0, 0, has_down), (1, 3, has_up)):
        @pl.when(side)
        def _(at=at, row=row):
            remote(hid.at[row, core], hid.at[row, core], hd_send.at[row], h_recv.at[at], chan=other).wait_recv()

        go(side, remote(hid.at[row, core], hid.at[row, core], hd_send.at[row], hd_recv.at[row], chan=other))
    wait_stats(1)
    make_norms(1, 4)
    for row in (1, 2, 0, 3):
        @pl.when(row_here(row))
        def _(row=row):
            remote(hid.at[row, core], hid.at[row, other], hd_send.at[row], hd_recv.at[row], chan=other).wait_recv()

    def norm2(step, carry):
        e, c = step // cores, step % cores
        shift = column(params[c, 4], local) - per_channel(means, step)
        gain = per_channel(scales, step) * column(params[c, 2], local)
        bias = column(params[c, 3], local)
        for row in range(4):
            v = hid[row, c, e].astype(F32)
            v = silu((v + shift) * gain + bias)
            v = jnp.where(row_here(row), v, 0.0)
            act2[pl.ds(pl.multiple_of(step * local, local), local), row * wide:(row + 1) * wide] = v.astype(BF16)
        return carry

    lax.fori_loop(0, 4 * cores, norm2, 0)

    bias2 = column(c2b[...], local)

    def conv2(o, carry):
        for r, h in enumerate(conv(act2, w2t, o)):
            mix[o * 2 + r] = latent[o, r].astype(F32) + (h + bias2)
        return carry

    lax.fori_loop(0, 2, conv2, 0)

    a, b = iota((2 * wide, 2 * wide), 0), iota((2 * wide, 2 * wide), 1)
    spread = jnp.where(b == 2 * (a % wide) + a // wide, 1.0, 0.0).astype(BF16)
    for f in range(2):
        for r in range(2):
            for p in range(2):
                pair = [mix[f * 2 + r, pl.ds(2 * p + q, local // 4, stride=4), :].astype(BF16) for q in range(2)]
                out[f, 2 * r + p] = jnp.dot(
                    jnp.concatenate(pair, axis=1), spread, preferred_element_type=F32
                ).astype(BF16)

    for condition, copy in started:
        @pl.when(condition)
        def _(copy=copy):
            copy.wait_send()


def shards(tiles, blocks, latent, n1g, n1b, w1, c1b, n2g, n2b, w2, c2b):
    frames, rows, local, wide = latent.shape
    count = tiles * blocks * 2
    groups = local // SIZE
    vmem = pl.BlockSpec(memory_space=pltpu.VMEM)
    hbm = pl.BlockSpec(memory_space=pl.ANY)
    dma = pltpu.SemaphoreType.DMA
    row = lambda v: v.reshape(1, local)
    return pl.pallas_call(
        functools.partial(kernel, tiles, blocks),
        out_shape=jax.ShapeDtypeStruct((frames, 2 * rows, local // 4, 2 * wide), BF16),
        in_specs=[vmem, vmem, vmem, hbm, vmem, vmem, vmem, hbm, vmem],
        out_specs=vmem,
        scratch_shapes=[
            pltpu.VMEM(w1.shape, BF16),
            pltpu.VMEM(w2.shape, BF16),
            pltpu.VMEM((3, 3 * local, 3 * C), BF16),
            pltpu.VMEM((3, 3 * local, 3 * C), BF16),
            pltpu.VMEM((3, 4, 2, 2, local, wide), BF16),
            pltpu.VMEM((6 * C, 4 * wide), BF16),
            pltpu.VMEM((4, 2, 4, local, wide), BF16),
            pltpu.VMEM((4 * C, 4 * wide), BF16),
            pltpu.VMEM((4, local, wide), F32),
            pltpu.VMEM((2, 5, 1, local), F32),
            pltpu.VMEM((2, 1, 128), F32),
            pltpu.VMEM((2, count, 1, 128), F32),
            pltpu.VMEM((12, groups, 128), F32),
            pltpu.VMEM((12, groups, 128), F32),
            dma((2,)),
            dma((2,)),
            dma((2, 2)),
            dma((3, 2)),
            dma((3, 4)),
            dma((3, 4)),
            dma((3, 4)),
            dma((2,)),
            dma((4,)),
            dma((2,)),
            dma((4,)),
            dma((2, count)),
            dma((2, count)),
        ],
        compiler_params=pltpu.CompilerParams(
            collective_id=0, has_side_effects=True, vmem_limit_bytes=48 * 1024 * 1024
        ),
        name="block",
    )(latent, row(n1g), row(n1b), w1, row(c1b), row(n2g), row(n2b), w2, row(c2b))


def solution(mesh):
    return jax.shard_map(
        functools.partial(shards, mesh.shape["tile"], mesh.shape["tm"]),
        mesh=mesh,
        in_specs=(
            P(("clip", "tm"), "tile", "chan", None),
            P("chan"),
            P("chan"),
            P(None, None, None, None, "chan"),
            P("chan"),
            P("chan"),
            P("chan"),
            P(None, None, None, None, "chan"),
            P("chan"),
        ),
        out_specs=P(("clip", "tm"), "tile", "chan", None),
        check_vma=False,
    )
```

time: 105 us -> 40 us (0.38)
  blocking collectives: 43.7 us -> 0 us
  Pallas kernels: 0 us -> 31.3 us
  waiting for transfers between devices: 27.4 us -> 0 us
  starting transfers between devices: 14.7 us -> 0 us
  matrix products: 6.68 us -> 0 us
  other arithmetic: 3.81 us -> 0 us
    pallas_call x0 -> x1, Pallas kernels: none -> 31.3 us  [shards(): pl.pallas_call(functools.partial(kernel, tiles, blocks), out_shape=jax.Sh...]
    ppermute x6 -> x0, waiting for transfers between devices: 27.4 us -> none  [the longest x2 11.6 us: passed_along(): lax.ppermute(value, axis, [(source, source + steps) for source in range(i...]
    psum x2 -> x0, blocking collectives: 22.3 us -> none  [causal_norm(): totals, squares = lax.psum((totals, squares), 'tile')]
    all_gather x6 -> x0, blocking collectives: 21.4 us -> none  [the longest x4 17.3 us: carried_in(): gathered = jax.tree.map(lambda a: lax.all_gather(a, axis), part)]
    ppermute x6 -> x0, starting transfers between devices: 14.7 us -> none  [the longest x2 7.4 us: passed_along(): lax.ppermute(value, axis, [(source, source + steps) for source in range(i...]
    dot_general x18 -> x0, matrix products: 6.68 us -> none  [causal_conv(): jnp.einsum('kfrcw,kcd->frdw', stacked, weight[depth_tap, row_tap], prefer...]
    unnamed x17 -> x19, local copies, waits for them, and re-layouts: 3.13 us -> 8.44 us
    another operation x10 -> x0, local copies, waits for them, and re-layouts: 2.01 us -> none  [the longest x6 2 us: causal_conv(): jnp.stack([slab[..., shift_tap:shift_tap + columns] for shift_tap in rang...]
  transfers between devices with their start and end apart: 6 -> 0, of which waited for: 6 -> 0; matrix products, arithmetic and copies ran while one was open for 0% -> 0% of each run, Pallas kernels for 0% -> 0%
where the time goes in v1:
time: 40 us; the launch traced here: 39.8 us
  Pallas kernels  31.3 us (78%)
  local copies, waits for them, and re-layouts  8.44 us (21%)
    pallas_call x1, Pallas kernels, shards(): pl.pallas_call(functools.partial(kernel, tiles, blocks), out_shape=jax.Sh...  31.3 us
    unnamed x19, local copies, waits for them, and re-layouts  8.44 us

profile of v1, /device:TPU:0, one launch (start us, length us, event | category | flops | bytes accessed | tf_op | source)
XLA Modules:
  0.0 39.8 jit_solution(1418587516966985887)
XLA Ops:
  0.0 0.0 copy-start
  0.0 1.5 %copy-done = bf16[3,3,3,256,128]{4,3,2,1,0:T(8,128)(2,1)S(1)} copy-done((bf16[3,3,3,256,128]{4,3,2,1,0:T(8,128)(2,1)S(1)}, bf16[3,3,3,256,128]{4,3,2,1,0:T(8,128)(2,1)}, u32[]{:S(2)}) %copy-start) | copy-done | bytes 1769496
  1.5 0.0 copy-start.1
  1.5 1.5 %copy-done.1 = bf16[3,3,3,256,128]{4,3,2,1,0:T(8,128)(2,1)S(1)} copy-done((bf16[3,3,3,256,128]{4,3,2,1,0:T(8,128)(2,1)S(1)}, bf16[3,3,3,256,128]{4,3,2,1,0:T(8,128)(2,1)}, u32[]{:S(2)}) %copy-start.1) | copy-done | bytes 1769496
  3.0 0.0 copy-start.2
  3.0 0.9 %copy-done.2 = bf16[2,2,128,128]{3,2,1,0:T(8,128)(2,1)S(1)} copy-done((bf16[2,2,128,128]{3,2,1,0:T(8,128)(2,1)S(1)}, bf16[2,2,128,128]{3,2,1,0:T(8,128)(2,1)}, u32[]{:S(2)}) %copy-start.2) | copy-done | bytes 131096
  3.9 0.0 copy-start.3
  3.9 0.7 %copy-done.3 = f32[128]{0:T(128)S(1)} copy-done((f32[128]{0:T(128)S(1)}, f32[128]{0:T(128)}, u32[]{:S(2)}) %copy-start.3) | copy-done | bytes 536
  4.5 0.0 copy-start.4
  4.5 0.7 %copy-done.4 = f32[128]{0:T(128)S(1)} copy-done((f32[128]{0:T(128)S(1)}, f32[128]{0:T(128)}, u32[]{:S(2)}) %copy-start.4) | copy-done | bytes 536
  5.2 0.0 copy-start.5
  5.2 0.7 %copy-done.5 = f32[128]{0:T(128)S(1)} copy-done((f32[128]{0:T(128)S(1)}, f32[128]{0:T(128)}, u32[]{:S(2)}) %copy-start.5) | copy-done | bytes 536
  5.8 0.0 copy-start.6
  5.8 0.7 %copy-done.6 = f32[128]{0:T(128)S(1)} copy-done((f32[128]{0:T(128)S(1)}, f32[128]{0:T(128)}, u32[]{:S(2)}) %copy-start.6) | copy-done | bytes 536
  6.5 0.0 copy-start.7
  6.5 0.7 %copy-done.7 = f32[128]{0:T(128)S(1)} copy-done((f32[128]{0:T(128)S(1)}, f32[128]{0:T(128)}, u32[]{:S(2)}) %copy-start.7) | copy-done | bytes 536
  7.1 0.0 copy-start.8
  7.1 0.7 %copy-done.8 = f32[128]{0:T(128)S(1)} copy-done((f32[128]{0:T(128)S(1)}, f32[128]{0:T(128)}, u32[]{:S(2)}) %copy-start.8) | copy-done | bytes 536
  7.8 31.3 %block.1 = bf16[2,4,32,256]{3,2,1,0:T(8,128)(2,1)S(1)} custom-call(bf16[2,2,128,128]{3,2,1,0:T(8,128)(2,1)S(1)} %copy-done.2, f32[1,128]{1,0:T(1,128)S(1)} %bitcast.6, f32[1,128]{1,0:T(1,128)S(1)} %bitcast.7, bf16[3,3,3,256,128]{4,3,2,1,0:T(8,128)(2,1)S(1)} %copy-done, f32[1,128]{1,0:T(1,128)S(1)} %bitcast.8, f32[1,128]{1,0:T(1,128)S(1)} %bitcast.9, ...), custom_call_target="tpu_custom_call" | custom-call | tf_op jit(solution)/shard_map/block/pallas_call | solution.py:375
  39.1 0.7 %copy.11 = bf16[2,4,32,256]{3,2,1,0:T(8,128)(2,1)} copy(bf16[2,4,32,256]{3,2,1,0:T(8,128)(2,1)S(1)} %block.1) | data formatting | bytes 262144
Async XLA Ops:
  0.0 1.5 %copy-start = (bf16[3,3,3,256,128]{4,3,2,1,0:T(8,128)(2,1)S(1)}, bf16[3,3,3,256,128]{4,3,2,1,0:T(8,128)(2,1)}, u32[]{:S(2)}) copy-start(bf16[3,3,3,256,128]{4,3,2,1,0:T(8,128)(2,1)} %w1.1) | copy-start | bytes 5308420
  1.5 1.5 %copy-start.1 = (bf16[3,3,3,256,128]{4,3,2,1,0:T(8,128)(2,1)S(1)}, bf16[3,3,3,256,128]{4,3,2,1,0:T(8,128)(2,1)}, u32[]{:S(2)}) copy-start(bf16[3,3,3,256,128]{4,3,2,1,0:T(8,128)(2,1)} %w2.1) | copy-start | bytes 5308420
  3.0 0.9 %copy-start.2 = (bf16[2,2,128,128]{3,2,1,0:T(8,128)(2,1)S(1)}, bf16[2,2,128,128]{3,2,1,0:T(8,128)(2,1)}, u32[]{:S(2)}) copy-start(bf16[2,2,128,128]{3,2,1,0:T(8,128)(2,1)} %latent.1) | copy-start | bytes 393220
  3.9 0.7 %copy-start.3 = (f32[128]{0:T(128)S(1)}, f32[128]{0:T(128)}, u32[]{:S(2)}) copy-start(f32[128]{0:T(128)} %param.10) | copy-start | bytes 1540
  4.5 0.7 %copy-start.4 = (f32[128]{0:T(128)S(1)}, f32[128]{0:T(128)}, u32[]{:S(2)}) copy-start(f32[128]{0:T(128)} %param.11) | copy-start | bytes 1540
  5.2 0.7 %copy-start.5 = (f32[128]{0:T(128)S(1)}, f32[128]{0:T(128)}, u32[]{:S(2)}) copy-start(f32[128]{0:T(128)} %param.13) | copy-start | bytes 1540
  5.8 0.7 %copy-start.6 = (f32[128]{0:T(128)S(1)}, f32[128]{0:T(128)}, u32[]{:S(2)}) copy-start(f32[128]{0:T(128)} %param.14) | copy-start | bytes 1540
  6.5 0.7 %copy-start.7 = (f32[128]{0:T(128)S(1)}, f32[128]{0:T(128)}, u32[]{:S(2)}) copy-start(f32[128]{0:T(128)} %param.15) | copy-start | bytes 1540
  7.1 0.7 %copy-start.8 = (f32[128]{0:T(128)S(1)}, f32[128]{0:T(128)}, u32[]{:S(2)}) copy-start(f32[128]{0:T(128)} %param.17) | copy-start | bytes 1540

commit v2 on v1

--- a/solution.py
+++ b/solution.py
@@ -51,6 +51,7 @@
     stats,
     means,
     scales,
+    l_sem,
     w_sem,
     p_sem,
     x_send,
@@ -80,11 +81,18 @@
     def where_is(index):
         return {"tm": index // (cores * tiles), "chan": (index // tiles) % cores, "tile": index % tiles}
 
+    def remote(src, dst, send, recv, **device):
+        return pltpu.make_async_remote_copy(
+            src_ref=src, dst_ref=dst, send_sem=send, recv_sem=recv, device_id=device, device_id_type=MESH
+        )
+
+    loads = [pltpu.make_async_copy(latent.at[:, r], lat.at[2, 1 + r, core], l_sem.at[r]) for r in (0, 1)]
+    loads += [
+        pltpu.make_async_copy(ref, params.at[core, i], l_sem.at[2 + i])
+        for i, ref in enumerate((n1g, n1b, n2g, n2b, c1b, c2b))
+    ]
     load1 = pltpu.make_async_copy(w1, w1v, w_sem.at[0])
     load2 = pltpu.make_async_copy(w2, w2v, w_sem.at[1])
-    load1.start()
-    load2.start()
-
     barrier = pltpu.get_barrier_semaphore()
 
     def greet(step, carry):
@@ -94,16 +102,12 @@
         return carry
 
     lax.fori_loop(1, count_all, greet, 0)
-    for i, ref in enumerate((n1g, n1b, n2g, n2b, c1b)):
-        params[core, i] = ref[...]
-    lat[2, 1, core] = latent[:, 0]
-    lat[2, 2, core] = latent[:, 1]
-    pl.semaphore_wait(barrier, count_all - 1)
-
-    def remote(src, dst, send, recv, **device):
-        return pltpu.make_async_remote_copy(
-            src_ref=src, dst_ref=dst, send_sem=send, recv_sem=recv, device_id=device, device_id_type=MESH
-        )
+    for copy in loads:
+        copy.start()
+    load1.start()
+    load2.start()
+    for copy in loads:
+        copy.wait()
 
     started = []
 
@@ -120,24 +124,13 @@
     slots = [s for s in range(3) if blocks > 2 - s]
     before = [s for s in slots if s < 2]
 
-    for s in reversed(before):
-        for r in (0, 1):
-            go(
-                tm + (2 - s) < blocks,
-                remote(latent.at[:, r], lat.at[s, 1 + r, core], x_send.at[s, r], a_recv.at[s, 1 + r],
-                       tm=tm + (2 - s)),
-            )
-    go(has_up, remote(latent.at[:, 1], lat.at[2, 0, core], z_send.at[2, 0], a_recv.at[2, 0], tile=tile + 1))
-    go(has_down, remote(latent.at[:, 0], lat.at[2, 3, core], z_send.at[2, 1], a_recv.at[2, 3], tile=tile - 1))
-    for r in (0, 1):
-        go(always, remote(latent.at[:, r], lat.at[2, 1 + r, core], d_send.at[2, 1 + r], d_recv.at[2, 1 + r],
-                          chan=other))
-    go(always, remote(params.at[core], params.at[core], p_sem.at[0], p_sem.at[1], chan=other))
+    def lat_copy(s, row, f, to_s, to_row, send, recv, **device):
+        return remote(lat.at[s, row, core, f], lat.at[to_s, to_row, core, f], send, recv, **device)
 
     lanes = iota((groups, 128), 1)
     subs = iota((groups, 128), 0)
 
-    def send_stats(which, field):
+    def make_stats(which, field):
         row = jnp.zeros((1, 128), F32)
         for f in (0, 1):
             total = jnp.zeros((groups, wide), F32)
@@ -153,6 +146,7 @@
         own_stats[which] = row
         stats[which, me] = row
 
+    def send_stats(which):
         def send(step, carry):
             to = lax.rem(me + step, count_all)
             remote(own_stats.at[which], stats.at[which, me], s_send.at[which, to], s_recv.at[which, me],
@@ -233,65 +227,121 @@
             result.append(a[1] + left + right)
         return result
 
-    send_stats(0, lambda f, r: latent[f, r].astype(F32))
+    make_stats(0, lambda f, r: lat[2, 1 + r, core, f].astype(F32))
+    pl.semaphore_wait(barrier, count_all - 1)
+    send_stats(0)
+
+    for s in reversed(before):
+        for f in (0, 1):
+            for r in (0, 1):
+                go(tm + (2 - s) < blocks,
+                   lat_copy(2, 1 + r, f, s, 1 + r, x_send.at[s, r, f], a_recv.at[s, 1 + r, f], tm=tm + (2 - s)))
+    for f in (0, 1):
+        go(has_up, lat_copy(2, 2, f, 2, 0, z_send.at[2, 0, f], a_recv.at[2, 0, f], tile=tile + 1))
+        go(has_down, lat_copy(2, 1, f, 2, 3, z_send.at[2, 1, f], a_recv.at[2, 3, f], tile=tile - 1))
+    for f in (0, 1):
+        for r in (1, 2):
+            go(always, lat_copy(2, r, f, 2, r, d_send.at[2, r, f], d_recv.at[2, r, f], chan=other))
+    go(always, remote(params.at[core], params.at[core], p_sem.at[0], p_sem.at[1], chan=other))
+
     load1.wait()
     flip(w1v, w1t)
-
-    def arrived(s, row, condition):
-        got = remote(lat.at[s, row, core], lat.at[s, row, core], d_send.at[s, row], a_recv.at[s, row], chan=other)
+    load2.wait()
+    flip(w2v, w2t)
+
+    def arrived(s, row, f, condition):
+        copy = lat_copy(s, row, f, s, row, d_send.at[s, row, f], d_recv.at[s, row, f], chan=other)
 
         @pl.when(condition)
         def _():
-            got.wait_recv()
-
-        go(condition, remote(lat.at[s, row, core], lat.at[s, row, core], d_send.at[s, row], d_recv.at[s, row],
-                             chan=other))
-
-    arrivals = []
+            lat_copy(s, row, f, s, row, d_send.at[s, row, f], a_recv.at[s, row, f], chan=other).wait_recv()
+            copy.start()
+
+        started.append((condition, copy))
+
+    def from_other(s, row, f, condition):
+        @pl.when(condition)
+        def _():
+            remote(lat.at[s, row, core, f], lat.at[s, row, other, f], d_send.at[s, row, f], d_recv.at[s, row, f],
+                   chan=other).wait_recv()
+
+    def row_here(row):
+        return has_down if row == 0 else has_up if row == 3 else always
+
+    for f in (0, 1):
+        for row in (0, 3):
+            arrived(2, row, f, row_here(row))
     for s in reversed(before):
         here = tm >= 2 - s
-        for r in (0, 1):
-            arrived(s, 1 + r, here)
-            side, row, to = ((has_down, 3, tile - 1), (has_up, 0, tile + 1))[r]
-            go(
-                jnp.logical_and(here, side),
-                remote(lat.at[s, 1 + r, core], lat.at[s, row, core], z_send.at[s, 1 - r], a_recv.at[s, row], tile=to),
-            )
-    for s in reversed(slots):
-        here = tm >= 2 - s
-        arrived(s, 0, jnp.logical_and(here, has_down))
-        arrived(s, 3, jnp.logical_and(here, has_up))
+        for f in (0, 1):
+            for r in (0, 1):
+                arrived(s, 1 + r, f, here)
+                side, row, to = ((has_down, 3, tile - 1), (has_up, 0, tile + 1))[r]
+                go(jnp.logical_and(here, side),
+                   lat_copy(s, 1 + r, f, s, row, z_send.at[s, 1 - r, f], a_recv.at[s, row, f], tile=to))
 
     wait_stats(0)
     make_norms(0, 6)
     remote(params.at[core], params.at[other], p_sem.at[0], p_sem.at[1], chan=other).wait_recv()
-
-    def row_here(row):
-        return has_down if row == 0 else has_up if row == 3 else always
-
-    for s in reversed(slots):
+    for f in (0, 1):
         for row in range(4):
-            @pl.when(jnp.logical_and(tm >= 2 - s, row_here(row)))
-            def _(s=s, row=row):
-                remote(lat.at[s, row, core], lat.at[s, row, other], d_send.at[s, row], d_recv.at[s, row],
-                       chan=other).wait_recv()
-
-    def norm1(step, carry):
-        e, c = step // cores, step % cores
-        s, f = e // 2, e % 2
-        f = jnp.where(tm - 2 + s < 0, 0, f)
-        s = jnp.maximum(s, 2 - tm)
-        mean = per_channel(means, step)
-        gain = per_channel(scales, step) * column(params[c, 0], local)
-        bias = column(params[c, 1], local)
-        for row in range(4):
-            v = lat[s, row, c, f].astype(F32)
-            v = silu((v - mean) * gain + bias)
-            v = jnp.where(row_here(row), v, 0.0)
-            act1[pl.ds(pl.multiple_of(step * local, local), local), row * wide:(row + 1) * wide] = v.astype(BF16)
-        return carry
-
-    lax.fori_loop(0, 6 * cores, norm1, 0)
+            from_other(2, row, f, row_here(row))
+
+    def norm1(first, rows_of):
+        def one(step, carry):
+            e, c = step // cores, step % cores
+            s, f = e // 2, e % 2
+            f = jnp.where(tm - 2 + s < 0, 0, f)
+            s = jnp.maximum(s, 2 - tm)
+            mean = per_channel(means, step)
+            gain = per_channel(scales, step) * column(params[c, 0], local)
+            bias = column(params[c, 1], local)
+            for row in rows_of:
+                v = lat[s, row, c, f].astype(F32)
+                v = silu((v - mean) * gain + bias)
+                if row in (0, 3):
+                    v = jnp.where(row_here(row), v, 0.0)
+                act1[pl.ds(pl.multiple_of(step * local, local), local), row * wide:(row + 1) * wide] = v.astype(BF16)
+            return carry
+
+        lax.fori_loop(first * cores, (first + 2) * cores, one, 0)
+
+    norm1(4, range(4))
+    for s in before:
+        for f in (0, 1):
+            for row in (0, 3):
+                arrived(s, row, f, jnp.logical_and(tm >= 2 - s, row_here(row)))
+    for s in before:
+        for f in (0, 1):
+            for row in (1, 2):
+                from_other(s, row, f, tm >= 2 - s)
+    norm1(2, (1, 2))
+    for s in before:
+        for f in (0, 1):
+            for row in (0, 3):
+                from_other(s, row, f, jnp.logical_and(tm >= 2 - s, row_here(row)))
+    norm1(2, (0, 3))
+
+    def repeat_first():
+        first = act1[2 * C:3 * C]
+        act1[0:C] = first
+        act1[C:2 * C] = first
+
+    if blocks > 2:
+        @pl.when(tm >= 2)
+        def _():
+            norm1(0, range(4))
+
+        pl.when(tm < 2)(repeat_first)
+    else:
+        repeat_first()
+
+    def z_copy(o, up):
+        at, row, to, landed = (0, 2, tile + 1, 0) if up else (1, 1, tile - 1, 3)
+        return remote(hid.at[row, core, o], hid.at[landed, core, o], hz_send.at[at, o], h_recv.at[at, o], tile=to)
+
+    def d_copy(o, row):
+        return remote(hid.at[row, core, o], hid.at[row, core, o], hd_send.at[row, o], hd_recv.at[row, o], chan=other)
 
     def conv1(o, carry):
         for r, h in enumerate(conv(act1, w1t, o)):
@@ -299,31 +349,33 @@
 
             @pl.when(o >= 2)
             def _():
-                mix[(o - 2) * 2 + r] = h
+                mix[jnp.maximum(o - 2, 0) * 2 + r] = h
+
+        pl.when(has_up)(lambda: z_copy(o, True).start())
+        pl.when(has_down)(lambda: z_copy(o, False).start())
+        d_copy(o, 1).start()
+        d_copy(o, 2).start()
         return carry
 
-    lax.fori_loop(0, 4, conv1, 0)
-
-    go(has_up, remote(hid.at[2, core], hid.at[0, core], hz_send.at[0], h_recv.at[0], tile=tile + 1))
-    go(has_down, remote(hid.at[1, core], hid.at[3, core], hz_send.at[1], h_recv.at[1], tile=tile - 1))
-    for r in (1, 2):
-        go(always, remote(hid.at[r, core], hid.at[r, core], hd_send.at[r], hd_recv.at[r], chan=other))
-    bias1 = column(c1b[...], local)
-    send_stats(1, lambda f, r: mix[f * 2 + r] + bias1)
-    load2.wait()
-    flip(w2v, w2t)
-    for at, row, side in ((0, 0, has_down), (1, 3, has_up)):
-        @pl.when(side)
-        def _(at=at, row=row):
-            remote(hid.at[row, core], hid.at[row, core], hd_send.at[row], h_recv.at[at], chan=other).wait_recv()
-
-        go(side, remote(hid.at[row, core], hid.at[row, core], hd_send.at[row], hd_recv.at[row], chan=other))
+    lax.fori_loop(2, 4, conv1, 0)
+    bias1 = column(params[core, 4], local)
+    make_stats(1, lambda f, r: mix[f * 2 + r] + bias1)
+    send_stats(1)
+    lax.fori_loop(0, 2, conv1, 0)
+
+    for o in (2, 3, 0, 1):
+        for at, row in ((0, 0), (1, 3)):
+            @pl.when(row_here(row))
+            def _(at=at, row=row, o=o):
+                remote(hid.at[row, core, o], hid.at[row, core, o], hd_send.at[row, o], h_recv.at[at, o],
+                       chan=other).wait_recv()
+                d_copy(o, row).start()
     wait_stats(1)
     make_norms(1, 4)
-    for row in (1, 2, 0, 3):
-        @pl.when(row_here(row))
-        def _(row=row):
-            remote(hid.at[row, core], hid.at[row, other], hd_send.at[row], hd_recv.at[row], chan=other).wait_recv()
+
+    def got(o, row):
+        remote(hid.at[row, core, o], hid.at[row, other, o], hd_send.at[row, o], hd_recv.at[row, o],
+               chan=other).wait_recv()
 
     def norm2(step, carry):
         e, c = step // cores, step % cores
@@ -333,17 +385,23 @@
         for row in range(4):
             v = hid[row, c, e].astype(F32)
             v = silu((v + shift) * gain + bias)
-            v = jnp.where(row_here(row), v, 0.0)
+            if row in (0, 3):
+                v = jnp.where(row_here(row), v, 0.0)
             act2[pl.ds(pl.multiple_of(step * local, local), local), row * wide:(row + 1) * wide] = v.astype(BF16)
         return carry
 
+    for o in (2, 3, 0, 1):
+        got(o, 1)
+        got(o, 2)
+        pl.when(has_down)(lambda o=o: got(o, 0))
+        pl.when(has_up)(lambda o=o: got(o, 3))
     lax.fori_loop(0, 4 * cores, norm2, 0)
 
-    bias2 = column(c2b[...], local)
+    bias2 = column(params[core, 5], local)
 
     def conv2(o, carry):
         for r, h in enumerate(conv(act2, w2t, o)):
-            mix[o * 2 + r] = latent[o, r].astype(F32) + (h + bias2)
+            mix[o * 2 + r] = lat[2, 1 + r, core, o].astype(F32) + (h + bias2)
         return carry
 
     lax.fori_loop(0, 2, conv2, 0)
@@ -362,6 +420,12 @@
         @pl.when(condition)
         def _(copy=copy):
             copy.wait_send()
+
+    for o in range(4):
+        pl.when(has_up)(lambda o=o: z_copy(o, True).wait_send())
+        pl.when(has_down)(lambda o=o: z_copy(o, False).wait_send())
+        for row in range(4):
+            pl.when(row_here(row))(lambda o=o, row=row: d_copy(o, row).wait_send())
 
 
 def shards(tiles, blocks, latent, n1g, n1b, w1, c1b, n2g, n2b, w2, c2b):
@@ -375,7 +439,7 @@
     return pl.pallas_call(
         functools.partial(kernel, tiles, blocks),
         out_shape=jax.ShapeDtypeStruct((frames, 2 * rows, local // 4, 2 * wide), BF16),
-        in_specs=[vmem, vmem, vmem, hbm, vmem, vmem, vmem, hbm, vmem],
+        in_specs=[hbm] * 9,
         out_specs=vmem,
         scratch_shapes=[
             pltpu.VMEM(w1.shape, BF16),
@@ -387,27 +451,28 @@
             pltpu.VMEM((4, 2, 4, local, wide), BF16),
             pltpu.VMEM((4 * C, 4 * wide), BF16),
             pltpu.VMEM((4, local, wide), F32),
-            pltpu.VMEM((2, 5, 1, local), F32),
+            pltpu.VMEM((2, 6, 1, local), F32),
             pltpu.VMEM((2, 1, 128), F32),
             pltpu.VMEM((2, count, 1, 128), F32),
             pltpu.VMEM((12, groups, 128), F32),
             pltpu.VMEM((12, groups, 128), F32),
+            dma((8,)),
             dma((2,)),
             dma((2,)),
-            dma((2, 2)),
-            dma((3, 2)),
-            dma((3, 4)),
-            dma((3, 4)),
-            dma((3, 4)),
-            dma((2,)),
-            dma((4,)),
-            dma((2,)),
-            dma((4,)),
+            dma((2, 2, 2)),
+            dma((3, 2, 2)),
+            dma((3, 4, 2)),
+            dma((3, 4, 2)),
+            dma((3, 4, 2)),
+            dma((2, 4)),
+            dma((4, 4)),
+            dma((2, 4)),
+            dma((4, 4)),
             dma((2, count)),
             dma((2, count)),
         ],
         compiler_params=pltpu.CompilerParams(
-            collective_id=0, has_side_effects=True, vmem_limit_bytes=48 * 1024 * 1024
+            collective_id=0, has_side_effects=True, vmem_limit_bytes=67_000_000
         ),
         name="block",
     )(latent, row(n1g), row(n1b), w1, row(c1b), row(n2g), row(n2b), w2, row(c2b))

time: 40 us -> 28.8 us (0.72)
  the two profiles are of different devices: /device:TPU:0 before, /device:TPU:3 now
where the time goes in v2:
time: 28.8 us; the launch traced here: 28.7 us
  Pallas kernels  27.1 us (94%)
  local copies, waits for them, and re-layouts  1.57 us (5%)
    pallas_call x1, Pallas kernels, shards(): pl.pallas_call(functools.partial(kernel, tiles, blocks), out_shape=jax.Sh...  27.1 us
    unnamed x1, local copies, waits for them, and re-layouts  1.57 us

profile of v2, /device:TPU:3, one launch (start us, length us, event | category | flops | bytes accessed | tf_op | source)
XLA Modules:
  0.0 28.7 jit_solution(14168829337476946724)
XLA Ops:
  0.0 27.1 %block.1 = bf16[2,4,32,256]{3,2,1,0:T(8,128)(2,1)} custom-call(bf16[2,2,128,128]{3,2,1,0:T(8,128)(2,1)} %latent.1, f32[1,128]{1,0:T(1,128)} %bitcast.6, f32[1,128]{1,0:T(1,128)} %bitcast.7, bf16[3,3,3,256,128]{4,3,2,1,0:T(8,128)(2,1)} %w1.1, f32[1,128]{1,0:T(1,128)} %bitcast.8, f32[1,128]{1,0:T(1,128)} %bitcast.9, f32[1,128]{1,0:T(1,128)} %bitcast.10, ...), custom_call_target="tpu_custom_call" | custom-call | tf_op jit(solution)/shard_map/block/pallas_call | solution.py:439
  27.1 1.6 %copy.11 = bf16[2,4,32,256]{3,2,1,0:T(8,128)(2,1)} copy(bf16[2,4,32,256]{3,2,1,0:T(8,128)(2,1)} %block.1) | data formatting | bytes 262144

commit v3 on v2

--- a/solution.py
+++ b/solution.py
@@ -46,6 +46,7 @@
     hid,
     act2,
     mix,
+    select,
     params,
     own_stats,
     stats,
@@ -206,9 +207,14 @@
 
         lax.fori_loop(0, 3, one, 0)
 
-    def silu(v):
-        half = 0.5 * v
+    def silu_of_twice(half):
         return half + half * jnp.tanh(half)
+
+    def clear_edges(act):
+        for side, row in ((has_down, 0), (has_up, 3)):
+            @pl.when(jnp.logical_not(side))
+            def _(row=row):
+                act[:, row * wide:(row + 1) * wide] = jnp.zeros((act.shape[0], wide), BF16)
 
     def conv(act, wt, o):
         acc = None
@@ -244,6 +250,8 @@
             go(always, lat_copy(2, r, f, 2, r, d_send.at[2, r, f], d_recv.at[2, r, f], chan=other))
     go(always, remote(params.at[core], params.at[core], p_sem.at[0], p_sem.at[1], chan=other))
 
+    a, b = iota((2 * wide, 2 * wide), 0), iota((2 * wide, 2 * wide), 1)
+    select[...] = jnp.where(b == 2 * (a % wide) + a // wide, 1.0, 0.0).astype(BF16)
     load1.wait()
     flip(w1v, w1t)
     load2.wait()
@@ -268,9 +276,6 @@
     def row_here(row):
         return has_down if row == 0 else has_up if row == 3 else always
 
-    for f in (0, 1):
-        for row in (0, 3):
-            arrived(2, row, f, row_here(row))
     for s in reversed(before):
         here = tm >= 2 - s
         for f in (0, 1):
@@ -280,6 +285,10 @@
                 go(jnp.logical_and(here, side),
                    lat_copy(s, 1 + r, f, s, row, z_send.at[s, 1 - r, f], a_recv.at[s, row, f], tile=to))
 
+    for f in (0, 1):
+        for row in (0, 3):
+            arrived(2, row, f, row_here(row))
+
     wait_stats(0)
     make_norms(0, 6)
     remote(params.at[core], params.at[other], p_sem.at[0], p_sem.at[1], chan=other).wait_recv()
@@ -293,14 +302,10 @@
             s, f = e // 2, e % 2
             f = jnp.where(tm - 2 + s < 0, 0, f)
             s = jnp.maximum(s, 2 - tm)
-            mean = per_channel(means, step)
-            gain = per_channel(scales, step) * column(params[c, 0], local)
-            bias = column(params[c, 1], local)
+            gain = per_channel(scales, step) * column(0.5 * params[c, 0], local)
+            bias = column(0.5 * params[c, 1], local) - per_channel(means, step) * gain
             for row in rows_of:
-                v = lat[s, row, c, f].astype(F32)
-                v = silu((v - mean) * gain + bias)
-                if row in (0, 3):
-                    v = jnp.where(row_here(row), v, 0.0)
+                v = silu_of_twice(lat[s, row, c, f].astype(F32) * gain + bias)
                 act1[pl.ds(pl.multiple_of(step * local, local), local), row * wide:(row + 1) * wide] = v.astype(BF16)
             return carry
 
@@ -336,6 +341,8 @@
     else:
         repeat_first()
 
+    clear_edges(act1)
+
     def z_copy(o, up):
         at, row, to, landed = (0, 2, tile + 1, 0) if up else (1, 1, tile - 1, 3)
         return remote(hid.at[row, core, o], hid.at[landed, core, o], hz_send.at[at, o], h_recv.at[at, o], tile=to)
@@ -377,25 +384,24 @@
         remote(hid.at[row, core, o], hid.at[row, other, o], hd_send.at[row, o], hd_recv.at[row, o],
                chan=other).wait_recv()
 
-    def norm2(step, carry):
+    def norm2(rows_of, step, carry):
         e, c = step // cores, step % cores
-        shift = column(params[c, 4], local) - per_channel(means, step)
-        gain = per_channel(scales, step) * column(params[c, 2], local)
-        bias = column(params[c, 3], local)
-        for row in range(4):
-            v = hid[row, c, e].astype(F32)
-            v = silu((v + shift) * gain + bias)
-            if row in (0, 3):
-                v = jnp.where(row_here(row), v, 0.0)
+        gain = per_channel(scales, step) * column(0.5 * params[c, 2], local)
+        bias = column(0.5 * params[c, 3], local) + (column(params[c, 4], local) - per_channel(means, step)) * gain
+        for row in rows_of:
+            v = silu_of_twice(hid[row, c, e].astype(F32) * gain + bias)
             act2[pl.ds(pl.multiple_of(step * local, local), local), row * wide:(row + 1) * wide] = v.astype(BF16)
         return carry
 
     for o in (2, 3, 0, 1):
         got(o, 1)
         got(o, 2)
+    lax.fori_loop(0, 4 * cores, functools.partial(norm2, (1, 2)), 0)
+    for o in (2, 3, 0, 1):
         pl.when(has_down)(lambda o=o: got(o, 0))
         pl.when(has_up)(lambda o=o: got(o, 3))
-    lax.fori_loop(0, 4 * cores, norm2, 0)
+    lax.fori_loop(0, 4 * cores, functools.partial(norm2, (0, 3)), 0)
+    clear_edges(act2)
 
     bias2 = column(params[core, 5], local)
 
@@ -406,8 +412,7 @@
 
     lax.fori_loop(0, 2, conv2, 0)
 
-    a, b = iota((2 * wide, 2 * wide), 0), iota((2 * wide, 2 * wide), 1)
-    spread = jnp.where(b == 2 * (a % wide) + a // wide, 1.0, 0.0).astype(BF16)
+    spread = select[...]
     for f in range(2):
         for r in range(2):
             for p in range(2):
@@ -435,7 +440,8 @@
     vmem = pl.BlockSpec(memory_space=pltpu.VMEM)
     hbm = pl.BlockSpec(memory_space=pl.ANY)
     dma = pltpu.SemaphoreType.DMA
-    row = lambda v: v.reshape(1, local)
+    here = lambda v: pltpu.with_memory_space_constraint(v, pltpu.HBM)
+    row = lambda v: here(v.reshape(1, local))
     return pl.pallas_call(
         functools.partial(kernel, tiles, blocks),
         out_shape=jax.ShapeDtypeStruct((frames, 2 * rows, local // 4, 2 * wide), BF16),
@@ -451,6 +457,7 @@
             pltpu.VMEM((4, 2, 4, local, wide), BF16),
             pltpu.VMEM((4 * C, 4 * wide), BF16),
             pltpu.VMEM((4, local, wide), F32),
+            pltpu.VMEM((2 * wide, 2 * wide), BF16),
             pltpu.VMEM((2, 6, 1, local), F32),
             pltpu.VMEM((2, 1, 128), F32),
             pltpu.VMEM((2, count, 1, 128), F32),
@@ -472,10 +479,10 @@
             dma((2, count)),
         ],
         compiler_params=pltpu.CompilerParams(
-            collective_id=0, has_side_effects=True, vmem_limit_bytes=67_000_000
+            collective_id=0, has_side_effects=True, vmem_limit_bytes=48 * 1024 * 1024
         ),
         name="block",
-    )(latent, row(n1g), row(n1b), w1, row(c1b), row(n2g), row(n2b), w2, row(c2b))
+    )(here(latent), row(n1g), row(n1b), here(w1), row(c1b), row(n2g), row(n2b), here(w2), row(c2b))
 
 
 def solution(mesh):

time: 28.8 us -> 27.6 us (0.958)
  the two profiles are of different devices: /device:TPU:3 before, /device:TPU:0 now
where the time goes in v3:
time: 27.6 us; the launch traced here: 27.4 us
  Pallas kernels  26.7 us (97%)
  local copies, waits for them, and re-layouts  0.66 us (2%)
    pallas_call x1, Pallas kernels, shards(): pl.pallas_call(functools.partial(kernel, tiles, blocks), out_shape=jax.Sh...  26.7 us
    unnamed x1, local copies, waits for them, and re-layouts  0.66 us

profile of v3, /device:TPU:0, one launch (start us, length us, event | category | flops | bytes accessed | tf_op | source)
XLA Modules:
  0.0 27.4 jit_solution(8373402654537232963)
XLA Ops:
  0.0 26.7 %block.1 = bf16[2,4,32,256]{3,2,1,0:T(8,128)(2,1)S(1)} custom-call(bf16[2,2,128,128]{3,2,1,0:T(8,128)(2,1)} %latent.1, f32[1,128]{1,0:T(1,128)} %bitcast.6, f32[1,128]{1,0:T(1,128)} %bitcast.7, bf16[3,3,3,256,128]{4,3,2,1,0:T(8,128)(2,1)} %w1.1, f32[1,128]{1,0:T(1,128)} %bitcast.8, f32[1,128]{1,0:T(1,128)} %bitcast.9, f32[1,128]{1,0:T(1,128)} %bitcast.10, ...), custom_call_target="tpu_custom_call" | custom-call | tf_op jit(solution)/shard_map/block/pallas_call | solution.py:445
  26.7 0.7 %copy.11 = bf16[2,4,32,256]{3,2,1,0:T(8,128)(2,1)} copy(bf16[2,4,32,256]{3,2,1,0:T(8,128)(2,1)S(1)} %block.1) | data formatting | bytes 262144

commit v4 on v3

--- a/solution.py
+++ b/solution.py
@@ -46,6 +46,7 @@
     hid,
     act2,
     mix,
+    mid,
     select,
     params,
     own_stats,
@@ -216,14 +217,21 @@
             def _(row=row):
                 act[:, row * wide:(row + 1) * wide] = jnp.zeros((act.shape[0], wide), BF16)
 
+    def tap(act, wt, o, j):
+        return jnp.dot(
+            wt[j], act[pl.ds(pl.multiple_of(o * C, C), 3 * C), j * wide:(j + 2) * wide],
+            preferred_element_type=F32,
+        )
+
+    def middle(act, wt, first, last):
+        def one(o, carry):
+            mid[o] = tap(act, wt, o, 1)
+            return carry
+
+        lax.fori_loop(first, last, one, 0)
+
     def conv(act, wt, o):
-        acc = None
-        for j in range(3):
-            part = jnp.dot(
-                wt[j], act[pl.ds(pl.multiple_of(o * C, C), 3 * C), j * wide:(j + 2) * wide],
-                preferred_element_type=F32,
-            )
-            acc = part if acc is None else acc + part
+        acc = mid[o] + tap(act, wt, o, 0) + tap(act, wt, o, 2)
         lane = iota((local, wide), 1)
         result = []
         for r in range(2):
@@ -311,36 +319,42 @@
 
         lax.fori_loop(first * cores, (first + 2) * cores, one, 0)
 
+    def norm1_first(rows_of):
+        def repeat():
+            for row in rows_of:
+                at = slice(row * wide, (row + 1) * wide)
+                first = act1[2 * C:3 * C, at]
+                act1[0:C, at] = first
+                act1[C:2 * C, at] = first
+
+        if blocks > 2:
+            @pl.when(tm >= 2)
+            def _():
+                norm1(0, rows_of)
+
+            pl.when(tm < 2)(repeat)
+        else:
+            repeat()
+
     norm1(4, range(4))
-    for s in before:
-        for f in (0, 1):
-            for row in (0, 3):
-                arrived(s, row, f, jnp.logical_and(tm >= 2 - s, row_here(row)))
     for s in before:
         for f in (0, 1):
             for row in (1, 2):
                 from_other(s, row, f, tm >= 2 - s)
     norm1(2, (1, 2))
+    norm1_first((1, 2))
+    middle(act1, w1t, 2, 4)
+    for s in before:
+        for f in (0, 1):
+            for row in (0, 3):
+                arrived(s, row, f, jnp.logical_and(tm >= 2 - s, row_here(row)))
+    middle(act1, w1t, 0, 2)
     for s in before:
         for f in (0, 1):
             for row in (0, 3):
                 from_other(s, row, f, jnp.logical_and(tm >= 2 - s, row_here(row)))
     norm1(2, (0, 3))
-
-    def repeat_first():
-        first = act1[2 * C:3 * C]
-        act1[0:C] = first
-        act1[C:2 * C] = first
-
-    if blocks > 2:
-        @pl.when(tm >= 2)
-        def _():
-            norm1(0, range(4))
-
-        pl.when(tm < 2)(repeat_first)
-    else:
-        repeat_first()
-
+    norm1_first((0, 3))
     clear_edges(act1)
 
     def z_copy(o, up):
@@ -397,6 +411,7 @@
         got(o, 1)
         got(o, 2)
     lax.fori_loop(0, 4 * cores, functools.partial(norm2, (1, 2)), 0)
+    middle(act2, w2t, 0, 2)
     for o in (2, 3, 0, 1):
         pl.when(has_down)(lambda o=o: got(o, 0))
         pl.when(has_up)(lambda o=o: got(o, 3))
@@ -457,6 +472,7 @@
             pltpu.VMEM((4, 2, 4, local, wide), BF16),
             pltpu.VMEM((4 * C, 4 * wide), BF16),
             pltpu.VMEM((4, local, wide), F32),
+            pltpu.VMEM((4, 3 * local, 2 * wide), F32),
             pltpu.VMEM((2 * wide, 2 * wide), BF16),
             pltpu.VMEM((2, 6, 1, local), F32),
             pltpu.VMEM((2, 1, 128), F32),

time: 27.6 us -> 27.7 us (level)
  no operation moved by 1% of the time
where the time goes in v4:
time: 27.7 us; the launch traced here: 27.5 us
  Pallas kernels  26.9 us (97%)
  local copies, waits for them, and re-layouts  0.66 us (2%)
    pallas_call x1, Pallas kernels, shards(): pl.pallas_call(functools.partial(kernel, tiles, blocks), out_shape=jax.Sh...  26.9 us
    unnamed x1, local copies, waits for them, and re-layouts  0.66 us

profile of v4, /device:TPU:0, one launch (start us, length us, event | category | flops | bytes accessed | tf_op | source)
XLA Modules:
  0.0 27.5 jit_solution(9290313429280810384)
XLA Ops:
  0.0 26.9 %block.1 = bf16[2,4,32,256]{3,2,1,0:T(8,128)(2,1)S(1)} custom-call(bf16[2,2,128,128]{3,2,1,0:T(8,128)(2,1)} %latent.1, f32[1,128]{1,0:T(1,128)} %bitcast.6, f32[1,128]{1,0:T(1,128)} %bitcast.7, bf16[3,3,3,256,128]{4,3,2,1,0:T(8,128)(2,1)} %w1.1, f32[1,128]{1,0:T(1,128)} %bitcast.8, f32[1,128]{1,0:T(1,128)} %bitcast.9, f32[1,128]{1,0:T(1,128)} %bitcast.10, ...), custom_call_target="tpu_custom_call" | custom-call | tf_op jit(solution)/shard_map/block/pallas_call | solution.py:460
  26.9 0.7 %copy.11 = bf16[2,4,32,256]{3,2,1,0:T(8,128)(2,1)} copy(bf16[2,4,32,256]{3,2,1,0:T(8,128)(2,1)S(1)} %block.1) | data formatting | bytes 262144

commit v5 on v4

--- a/solution.py
+++ b/solution.py
@@ -70,6 +70,7 @@
 ):
     cores = 2
     count_all = tiles * blocks * cores
+    few = count_all <= 16
     tm = lax.axis_index("tm")
     tile = lax.axis_index("tile")
     core = lax.axis_index("chan")
@@ -103,7 +104,7 @@
         )
         return carry
 
-    lax.fori_loop(1, count_all, greet, 0)
+    lax.fori_loop(1, count_all, greet, 0, unroll=few)
     for copy in loads:
         copy.start()
     load1.start()
@@ -155,7 +156,7 @@
                    **where_is(to)).start()
             return carry
 
-        lax.fori_loop(1, count_all, send, 0)
+        lax.fori_loop(1, count_all, send, 0, unroll=few)
 
     def wait_stats(which):
         def wait(step, carry):
@@ -164,7 +165,7 @@
                    **where_is(to)).wait()
             return carry
 
-        lax.fori_loop(1, count_all, wait, 0)
+        lax.fori_loop(1, count_all, wait, 0, unroll=few)
 
     def make_norms(which, frames):
         ahead = frames // 2 - 1

time: 27.7 us -> 27.7 us (level)
  no operation moved by 1% of the time
where the time goes in v5:
time: 27.7 us; the launch traced here: 27.6 us
  Pallas kernels  26.9 us (97%)
  local copies, waits for them, and re-layouts  0.66 us (2%)
    pallas_call x1, Pallas kernels, shards(): pl.pallas_call(functools.partial(kernel, tiles, blocks), out_shape=jax.Sh...  26.9 us
    unnamed x1, local copies, waits for them, and re-layouts  0.66 us

profile of v5, /device:TPU:0, one launch (start us, length us, event | category | flops | bytes accessed | tf_op | source)
XLA Modules:
  0.0 27.6 jit_solution(17509214524339309159)
XLA Ops:
  0.0 26.9 %block.1 = bf16[2,4,32,256]{3,2,1,0:T(8,128)(2,1)S(1)} custom-call(bf16[2,2,128,128]{3,2,1,0:T(8,128)(2,1)} %latent.1, f32[1,128]{1,0:T(1,128)} %bitcast.6, f32[1,128]{1,0:T(1,128)} %bitcast.7, bf16[3,3,3,256,128]{4,3,2,1,0:T(8,128)(2,1)} %w1.1, f32[1,128]{1,0:T(1,128)} %bitcast.8, f32[1,128]{1,0:T(1,128)} %bitcast.9, f32[1,128]{1,0:T(1,128)} %bitcast.10, ...), custom_call_target="tpu_custom_call" | custom-call | tf_op jit(solution)/shard_map/block/pallas_call | solution.py:461
  26.9 0.7 %copy.11 = bf16[2,4,32,256]{3,2,1,0:T(8,128)(2,1)} copy(bf16[2,4,32,256]{3,2,1,0:T(8,128)(2,1)S(1)} %block.1) | data formatting | bytes 262144
